TPU v7x, 128 devices: a whole 4x4x4 slice. The times are simulated.
128 devices in a mesh: group: 4 (over y), ctx: 32 (over x, z, core).
Axes of the slice: x: 4, y: 4, z: 4, core: 2. Of those that a mesh axis runs over, the one named last changes fastest.
Arguments:
- query: bfloat16 [128, 128, 576], P('group', 'ctx'), may hold values from -160 to 160
- cache: bfloat16 [32, 32768, 576], P('group', 'ctx'), may hold values from -6 to 6
- new_keys: bfloat16 [128, 576], P('group'), may hold values from -7 to 7
- lengths: int32 [32], P('group'), may hold values from 1 to 32768, as said below
- value_up_weight: bfloat16 [128, 512, 128], P('ctx'), may hold values from -1 to 1
- w_out: bfloat16 [16384, 7168], P('ctx'), may hold values from -0.1875 to 0.1875
- residual: bfloat16 [128, 7168], P(('group', 'ctx')), may hold values from -6 to 6
- norm_gain: float32 [7168], replicated, may hold values from 0.1 to 1.9
- w_router: bfloat16 [7168, 16], replicated, may hold values from -0.125 to 0.125
- routes: int32 [128, 8], P(('group', 'ctx')), may hold values from 0 to 15, all different within a row
- w_gate: bfloat16 [7168, 32768], P(None, ('group', 'ctx')), may hold values from -0.0625 to 0.0625
- w_up: bfloat16 [7168, 32768], P(None, ('group', 'ctx')), may hold values from -0.0625 to 0.0625
- w_down: bfloat16 [32768, 7168], P(('group', 'ctx')), may hold values from -0.125 to 0.125
Outputs:
- attn_out: bfloat16 [128, 7168], P(('group', 'ctx'))
- layer_out: bfloat16 [128, 7168], P(('group', 'ctx'))
Inputs may be any that keep to these rules, and one draw needn't show every extreme that they name: `lengths`: some request has all 32768 positions live.
All inputs are finite; a program needn't handle non-finite values.
Results may differ from a plain program's by a relative error of at most 0.018.
Values may be sent and summed in bfloat16 or wider, within the bound.
No kernel may reach another device: no remote copies, remote signals or barrier semaphores. Data moves between devices by JAX's collectives and lax.ppermute only.
A program may use at most 192 MiB of HBM per device.

v0:
```python
import jax
import jax.numpy as jnp
from jax import lax
from jax.sharding import PartitionSpec as P

LATENT_WIDTH = 512
ROTARY_WIDTH = 64
QK_NOPE = 128
VALUE_HEAD_WIDTH = 128
EXPERTS = 16
neg_floor = -1e30
route_scale = 2.5
norm_eps = 1e-06


def expert_partial(slot_rows, w_gate, w_up, w_down):
    gate_sum = jnp.dot(slot_rows, w_gate, preferred_element_type=jnp.float32)
    up_sum = jnp.dot(slot_rows, w_up, preferred_element_type=jnp.float32)
    hidden = (jax.nn.silu(gate_sum) * up_sum).astype(jnp.bfloat16)
    return jnp.dot(hidden, w_down, preferred_element_type=jnp.float32)


def local(
    query,
    cache,
    new_keys,
    lengths,
    value_up_weight,
    w_out,
    residual,
    norm_gain,
    w_router,
    routes,
    w_gate,
    w_up,
    w_down,
):
    score_scale = (QK_NOPE + ROTARY_WIDTH) ** (-0.5)
    ctx_count = lax.axis_size("ctx")
    group_count = lax.axis_size("group")
    ctx_index = lax.axis_index("ctx")
    grouped_rows, local_heads, features = query.shape
    request_batch = lengths.shape[0]
    draft_tokens = grouped_rows // request_batch
    block_len = cache.shape[1]
    positions = ctx_index * block_len + jnp.arange(block_len, dtype=jnp.int32)
    live_mask = (positions[None, :] < lengths[:, None])[:, None, None, :]
    compressed_keys = cache[:, :, :LATENT_WIDTH]
    all_heads = lax.all_gather(query, "ctx", axis=1, tiled=True)
    current_width = all_heads.shape[1]
    shaped = all_heads.reshape(request_batch, draft_tokens, current_width, features)
    scores = score_scale * jnp.einsum(
        "rqhd,rtd->rqht", shaped, cache, preferred_element_type=jnp.float32
    )
    block_max = jnp.max(jnp.where(live_mask, scores, neg_floor), axis=-1)
    probability = jnp.exp(jnp.where(live_mask, scores - block_max[..., None], neg_floor))
    block_sum = jnp.sum(probability, axis=-1)
    block_result = jnp.einsum(
        "rqht,rtk->rqhk",
        probability.astype(jnp.bfloat16),
        compressed_keys,
        preferred_element_type=jnp.float32,
    )
    arrived = (
        lax.all_to_all(
            block_max.reshape(grouped_rows, current_width)[None],
            "ctx",
            split_axis=2,
            concat_axis=0,
            tiled=True,
        ),
        lax.all_to_all(
            block_sum.reshape(grouped_rows, current_width)[None],
            "ctx",
            split_axis=2,
            concat_axis=0,
            tiled=True,
        ),
        lax.all_to_all(
            block_result.reshape(grouped_rows, current_width, LATENT_WIDTH)[None],
            "ctx",
            split_axis=2,
            concat_axis=0,
            tiled=True,
        ),
    )
    cache_max = jnp.max(arrived[0], axis=0)
    factors = jnp.exp(arrived[0] - cache_max[None])
    cache_sum = jnp.sum(factors * arrived[1], axis=0)
    cache_result = jnp.sum(factors[..., None] * arrived[2], axis=0)
    own_query = query.reshape(request_batch, draft_tokens, local_heads, features)
    recent_keys = new_keys.reshape(request_batch, draft_tokens, features)
    near_scores = score_scale * jnp.einsum(
        "rqhd,rjd->rqhj", own_query, recent_keys, preferred_element_type=jnp.float32
    )
    causal = (
        jnp.arange(draft_tokens, dtype=jnp.int32)[None, :]
        <= jnp.arange(draft_tokens, dtype=jnp.int32)[:, None]
    )
    causal = causal[None, :, None, :]
    near_max = jnp.max(jnp.where(causal, near_scores, neg_floor), axis=-1)
    shaped_max = cache_max.reshape(request_batch, draft_tokens, local_heads)
    joint_max = jnp.maximum(shaped_max, near_max)
    cache_rescale = jnp.exp(shaped_max - joint_max)
    nearby_probability = jnp.exp(jnp.where(causal, near_scores - joint_max[..., None], neg_floor))
    denominator = cache_sum.reshape(
        request_batch, draft_tokens, local_heads
    ) * cache_rescale + jnp.sum(nearby_probability, axis=-1)
    softmax_numerator = cache_result.reshape(
        request_batch, draft_tokens, local_heads, LATENT_WIDTH
    ) * cache_rescale[..., None] + jnp.einsum(
        "rqhj,rjk->rqhk",
        nearby_probability,
        recent_keys[:, :, :LATENT_WIDTH].astype(jnp.float32),
        precision=lax.Precision.HIGHEST,
    )
    latent_vector = (
        (softmax_numerator / denominator[..., None])
        .astype(jnp.bfloat16)
        .reshape(grouped_rows, local_heads, LATENT_WIDTH)
    )
    per_head_values = jnp.einsum(
        "gxj,xjs->gxs", latent_vector, value_up_weight, preferred_element_type=jnp.float32
    )
    per_head_values = per_head_values.astype(jnp.bfloat16).reshape(
        grouped_rows, local_heads * VALUE_HEAD_WIDTH
    )
    row_count = residual.shape[0]
    attention = lax.psum_scatter(
        jnp.dot(per_head_values, w_out, preferred_element_type=jnp.float32).astype(jnp.bfloat16),
        "ctx",
        scatter_dimension=0,
        tiled=True,
    ).astype(jnp.float32)
    attn_out = attention.astype(jnp.bfloat16)
    stream = (residual.astype(jnp.float32) + attention).astype(jnp.bfloat16)
    stream_wide = stream.astype(jnp.float32)
    mean_square = jnp.mean(stream_wide * stream_wide, axis=-1, keepdims=True)
    normed = (stream_wide * lax.rsqrt(mean_square + norm_eps) * norm_gain).astype(jnp.bfloat16)
    gate_values = jax.nn.sigmoid(jnp.dot(normed, w_router, preferred_element_type=jnp.float32))
    expert_ids = jnp.arange(EXPERTS, dtype=jnp.int32)
    selected_experts = (routes[:, :, None] == expert_ids[None, None, :]).astype(jnp.float32)
    picked = jnp.sum(selected_experts * gate_values[:, None, :], axis=-1)
    route_weights = route_scale * picked / jnp.sum(picked, axis=-1, keepdims=True)
    device_count = group_count * ctx_count
    slices = device_count // EXPERTS
    owners = jnp.arange(device_count, dtype=jnp.int32) // slices
    row_ids = jnp.arange(row_count, dtype=jnp.int32)
    earlier = row_ids[:, None] > row_ids[None, :]
    same_expert = routes[:, :, None, None] == routes[None, None, :, :]
    slot_index = jnp.sum((same_expert & earlier[:, None, :, None]).astype(jnp.int32), axis=(2, 3))
    targets = (routes[:, :, None] == owners[None, None, :])[..., None] & (
        slot_index[:, :, None, None] == row_ids[None, None, None, :]
    )
    placing = jnp.sum(targets.astype(jnp.float32), axis=1)
    coefficient = jnp.sum(route_weights[:, :, None, None] * targets.astype(jnp.float32), axis=1)
    outgoing = jnp.einsum(
        "idc,ij->dcj", placing.astype(jnp.bfloat16), normed, preferred_element_type=jnp.float32
    ).astype(jnp.bfloat16)
    model_width = residual.shape[1]
    slot_block = lax.all_to_all(outgoing, ("group", "ctx"), split_axis=0, concat_axis=0, tiled=True)
    slot_span = slot_block.shape[1]
    partial_out = expert_partial(
        slot_block.reshape(device_count * slot_span, model_width), w_gate, w_up, w_down
    )
    returned = lax.all_to_all(
        partial_out.reshape(device_count, slot_span, model_width).astype(jnp.bfloat16),
        ("group", "ctx"),
        split_axis=0,
        concat_axis=0,
        tiled=True,
    ).astype(jnp.float32)
    expert_mix = jnp.einsum("idc,dcj->ij", coefficient, returned, precision=lax.Precision.HIGHEST)
    layer_out = (stream_wide + expert_mix).astype(jnp.bfloat16)
    return (attn_out, layer_out)


def solution(mesh):
    return jax.shard_map(
        local,
        mesh=mesh,
        in_specs=(
            P("group", "ctx", None),
            P("group", "ctx", None),
            P("group", None),
            P("group"),
            P("ctx", None, None),
            P("ctx", None),
            P(("group", "ctx"), None),
            P(),
            P(),
            P(("group", "ctx"), None),
            P(None, ("group", "ctx")),
            P(None, ("group", "ctx")),
            P(("group", "ctx"), None),
        ),
        out_specs=(P(("group", "ctx"), None), P(("group", "ctx"), None)),
        check_vma=False,
    )
```

profile of v0, /device:TPU:1, one launch (start us, length us, event | category | flops | bytes accessed | tf_op | source)
XLA Modules:
  0.0 506.6 jit_solution(4167287995145306483)
XLA Ops:
  7.2 1.6 copy.86
  8.9 0.7 broadcast_compare_fusion
  9.6 51.8 %all-gather.2.cloned.1.call-done = bf16[32,128,576]{2,0,1:T(8,128)(2,1)} async-done(((bf16[32,4,576]{2,0,1:T(8,128)(2,1)}), bf16[32,128,576]{2,0,1:T(8,128)(2,1)}) %all-gather.2.cloned.1.call-update) | async-done | bytes 4718608 | tf_op jit(solution)/shard_map/all_gather | solution.py:49
  61.5 8.7 %copy.87 = bf16[32,128,576]{1,2,0:T(8,128)(2,1)} copy(bf16[32,128,576]{2,0,1:T(8,128)(2,1)} %all-gather.2.cloned.1.call-done) | data formatting | bytes 9437184 | tf_op jit(solution)/shard_map/all_gather | solution.py:49
  70.1 10.9 %select_reduce_fusion = (f32[8,4,128]{2,1,0:T(4,128)S(1)}, f32[8,4,128,1024]{3,2,1,0:T(8,128)S(1)}) fusion(pred[8,1024]{1,0:T(8,128)(4,1)S(1)} %broadcast_compare_fusion, bf16[8,4,128,576]{2,3,1,0:T(8,128)(2,1)} %bitcast.110, bf16[8,1024,576]{1,2,0:T(8,128)(2,1)} %param.14), kind=kOutput, calls=%fused_computation.1 | convolution fusion | flops 4844417024 | bytes 30957568 | tf_op jit(solution)/shard_map/rqhd,rtd->rqht/dot_general | solution.py:52
  81.1 4.4 fusion
  85.5 1.3 copy-done.1
  86.9 0.5 broadcast.318
  87.4 0.8 reduce.9
  88.2 0.7 reshape.421
  88.9 5.3 %all-to-all-start.2 = ((f32[32,1,128]{2,1,0:T(1,128)}), f32[32,1,128]{2,1,0:T(1,128)S(1)}, u32[]{:S(2)}, u32[]{:S(2)}) async-start(f32[32,1,128]{2,1,0:T(1,128)} %reshape.421), calls=%async_computation.2 | async-start | bytes 32768 | tf_op jit(solution)/shard_map/all_to_all | solution.py:72
  94.3 0.8 reduce.11
  95.1 0.7 reshape.419
  95.8 5.3 %all-to-all-done.2 = f32[32,1,128]{2,1,0:T(1,128)S(1)} async-done(((f32[32,1,128]{2,1,0:T(1,128)}), f32[32,1,128]{2,1,0:T(1,128)S(1)}, u32[]{:S(2)}, u32[]{:S(2)}) %all-to-all-start.2) | async-done | bytes 16416 | tf_op jit(solution)/shard_map/all_to_all | solution.py:72
  101.1 4.1 all-to-all-start
  105.2 13.0 %fusion.4 = f32[8,4,128,512]{3,2,1,0:T(8,128)} fusion(f32[8,4,128,1024]{3,2,1,0:T(8,128)} %copy-done.1, bf16[8,1024,576]{1,2,0:T(8,128)(2,1)} %param.14, f32[8,4,128]{2,1,0:T(4,128)S(1)} %get-tuple-element.13, pred[8,1024]{1,0:T(8,128)(4,1)S(1)} %broadcast_compare_fusion), kind=kOutput, calls=%fused_computation.7 | convolution fusion | flops 4311744512 | bytes 33579008 | tf_op jit(solution)/shard_map/rqht,rtk->rqhk/dot_general | solution.py:58
  118.2 11.5 %copy.90 = f32[1,32,128,512]{3,1,0,2:T(8,128)} copy(f32[1,32,128,512]{3,2,1,0:T(8,128)} %bitcast.109) | data formatting | bytes 16777216 | tf_op jit(solution)/shard_map/broadcast_in_dim;reshape | solution.py:80
  129.7 7.7 %all-to-all-start.1 = ((f32[1,32,128,512]{3,1,0,2:T(8,128)}), f32[1,32,128,512]{3,1,0,2:T(8,128)}, u32[]{:S(2)}, u32[]{:S(2)}) async-start(f32[1,32,128,512]{3,1,0,2:T(8,128)} %copy.90), calls=%async_computation.1 | async-start | bytes 16777216 | tf_op jit(solution)/shard_map/all_to_all | solution.py:79
  137.4 0.3 all-reduce.3.cloned.1.call-start
  137.7 1.0 select_reduce_fusion.1
  138.7 0.7 reduce.10
  139.4 0.1 reshape.422
  139.6 0.7 reduce.12
  140.8 105.1 %all-to-all-done.1 = f32[1,32,128,512]{3,1,0,2:T(8,128)} async-done(((f32[1,32,128,512]{3,1,0,2:T(8,128)}), f32[1,32,128,512]{3,1,0,2:T(8,128)}, u32[]{:S(2)}, u32[]{:S(2)}) %all-to-all-start.1) | async-done | bytes 8388640 | tf_op jit(solution)/shard_map/all_to_all | solution.py:79
  245.9 3.8 multiply_reduce_fusion
  249.8 0.2 copy.91
  250.0 0.5 fusion.22
  250.5 0.2 fusion.29
  250.8 5.3 %convolution_convert_fusion.1 = bf16[32,7168]{1,0:T(8,128)(2,1)} fusion(bf16[512,7168]{1,0:T(8,128)(2,1)} %param.18, bf16[4,4,8,128]{3,2,1,0:T(8,128)(2,1)S(1)} %fusion.29), kind=kOutput, calls=%fused_computation.16 | convolution fusion | flops 235110400 | bytes 7831552 | tf_op jit(solution)/shard_map/dot_general | solution.py:130
  256.1 0.6 dynamic-slice
  256.7 117.4 %all-reduce.3.cloned.1.call-done = bf16[32,7168]{1,0:T(8,128)(2,1)} async-done(((bf16[32,7168]{1,0:T(8,128)(2,1)}), bf16[32,7168]{1,0:T(8,128)(2,1)}) %all-reduce.3.cloned.1.call-update) | async-done | bytes 458768
  374.1 2.8 multiply_reduce_fusion.2
  377.7 0.2 fusion.33
  377.9 0.7 select_reduce_fusion.2
  378.6 0.6 multiply_divide_fusion
  379.4 0.3 fusion.14
  379.7 0.5 broadcast.322
  380.2 2.7 reduce.13
  382.9 4.6 reshape.423
  387.5 35.5 %all_to_all.64 = bf16[128,2,3584]{2,1,0:T(2,128)(2,1)} all-to-all(bf16[128,2,3584]{2,1,0:T(2,128)(2,1)S(1)} %reshape.423), channel_id=1, replica_groups=mesh['group'=4,'ctx'=32] {'group','ctx'}, dimensions={0} | all-to-all | bytes 3670016 | tf_op jit(solution)/shard_map/all_to_all | solution.py:161
  423.0 11.5 %reshape.424 = bf16[128,1,7168]{2,1,0:T(2,128)(2,1)} reshape(bf16[128,2,3584]{2,1,0:T(2,128)(2,1)} %all_to_all.64) | data formatting | bytes 3670016
  434.5 3.9 fusion.19
  438.5 6.3 %fusion.12 = bf16[128,1,7168]{2,0,1:T(8,128)(2,1)S(1)} fusion(bf16[256,7168]{1,0:T(8,128)(2,1)} %param.25, bf16[7168,256]{1,0:T(8,128)(2,1)} %param.24, bf16[128,1,7168]{2,1,0:T(2,128)(2,1)} %reshape.424, f32[128,256]{1,0:T(8,128)S(1)} %fusion.19), kind=kOutput, calls=%fused_computation.15 | convolution fusion | flops 940638208 | bytes 11141120 | tf_op jit(solution)/shard_map/dot_general | solution.py:20
  444.8 2.7 reduce.14
  447.5 4.6 reshape.425
  452.1 32.3 %all_to_all.65 = bf16[128,2,3584]{2,1,0:T(2,128)(2,1)} all-to-all(bf16[128,2,3584]{2,1,0:T(2,128)(2,1)S(1)} %reshape.425), channel_id=1, replica_groups=mesh['group'=4,'ctx'=32] {'group','ctx'}, dimensions={0} | all-to-all | bytes 3670016 | tf_op jit(solution)/shard_map/all_to_all | solution.py:166
  484.4 11.5 %reshape.426 = bf16[128,1,7168]{2,1,0:T(2,128)(2,1)} reshape(bf16[128,2,3584]{2,1,0:T(2,128)(2,1)} %all_to_all.65) | data formatting | bytes 3670016
  495.9 3.8 fusion.13
  (40 shorter events, 1.1 us)
Async XLA Ops:
  7.2 243.3 %copy-start = (bf16[4,512,128]{2,1,0:T(8,128)(2,1)S(1)}, bf16[4,512,128]{2,1,0:T(8,128)(2,1)}, u32[]{:S(2)}) copy-start(bf16[4,512,128]{2,1,0:T(8,128)(2,1)} %param.17) | copy-start | bytes 1572868
  7.2 54.3 %all-gather.2.cloned.1.call-start = ((), (), s32[]{:S(2)}) async-start(), calls=%async_computation.5 | async-start | bytes 5406720 | tf_op jit(solution)/shard_map/all_gather | solution.py:49
  81.1 5.7 %copy-start.1 = (f32[8,4,128,1024]{3,2,1,0:T(8,128)}, f32[8,4,128,1024]{3,2,1,0:T(8,128)S(1)}, u32[]{:S(2)}) copy-start(f32[8,4,128,1024]{3,2,1,0:T(8,128)S(1)} %get-tuple-element.14) | copy-start | bytes 50331652
  88.9 12.1 %all-to-all-start.2 = ((f32[32,1,128]{2,1,0:T(1,128)}), f32[32,1,128]{2,1,0:T(1,128)S(1)}, u32[]{:S(2)}, u32[]{:S(2)}) async-start(f32[32,1,128]{2,1,0:T(1,128)} %reshape.421), calls=%async_computation.2 | async-start | bytes 32768 | tf_op jit(solution)/shard_map/all_to_all | solution.py:72
  101.1 28.6 %all-to-all-start = ((f32[32,1,128]{2,1,0:T(1,128)}), f32[32,1,128]{2,1,0:T(1,128)S(1)}, u32[]{:S(2)}, u32[]{:S(2)}) async-start(f32[32,1,128]{2,1,0:T(1,128)} %reshape.419), calls=%async_computation | async-start | bytes 32768 | tf_op jit(solution)/shard_map/all_to_all | solution.py:65
  129.7 8.0 %copy-start.3 = (bf16[32,576]{1,0:T(8,128)(2,1)S(1)}, bf16[32,576]{1,0:T(8,128)(2,1)}, u32[]{:S(2)}) copy-start(bf16[32,576]{1,0:T(8,128)(2,1)} %param.15) | copy-start | bytes 110596
  129.7 8.0 %copy-start.2 = (bf16[32,4,576]{2,1,0:T(4,128)(2,1)S(1)}, bf16[32,4,576]{2,1,0:T(4,128)(2,1)}, u32[]{:S(2)}) copy-start(bf16[32,4,576]{2,1,0:T(4,128)(2,1)} %param.13) | copy-start | bytes 442372
  129.7 116.2 %all-to-all-start.1 = ((f32[1,32,128,512]{3,1,0,2:T(8,128)}), f32[1,32,128,512]{3,1,0,2:T(8,128)}, u32[]{:S(2)}, u32[]{:S(2)}) async-start(f32[1,32,128,512]{3,1,0,2:T(8,128)} %copy.90), calls=%async_computation.1 | async-start | bytes 16777216 | tf_op jit(solution)/shard_map/all_to_all | solution.py:79
  137.4 236.7 %all-reduce.3.cloned.1.call-start = ((), (), s32[]{:S(2)}) async-start(), calls=%async_computation.6 | async-start | bytes 917504
  250.7 5.4 %copy-start.8 = (u32[128]{0:T(128)S(1)}, u32[128]{0:T(128)}, u32[]{:S(2)}) copy-start(u32[128]{0:T(128)} %constant.59) | copy-start | bytes 1540
  250.7 123.4 %copy-start.4 = (bf16[1,7168]{1,0:T(2,128)(2,1)S(1)}, bf16[1,7168]{1,0:T(2,128)(2,1)}, u32[]{:S(2)}) copy-start(bf16[1,7168]{1,0:T(2,128)(2,1)} %param.19) | copy-start | bytes 43012
  250.7 126.9 %copy-start.5 = (f32[7168]{0:T(1024)S(1)}, f32[7168]{0:T(1024)}, u32[]{:S(2)}) copy-start(f32[7168]{0:T(1024)} %param.20) | copy-start | bytes 86020
  250.7 127.0 %copy-start.7 = (bf16[7168,16]{0,1:T(8,128)(2,1)S(1)}, bf16[7168,16]{0,1:T(8,128)(2,1)}, u32[]{:S(2)}) copy-start(bf16[7168,16]{0,1:T(8,128)(2,1)} %param.21) | copy-start | bytes 688132
  250.8 127.2 %copy-start.6 = (s32[1,8]{1,0:T(1,128)S(1)}, s32[1,8]{1,0:T(1,128)}, u32[]{:S(2)}) copy-start(s32[1,8]{1,0:T(1,128)} %param.22) | copy-start | bytes 100
Sparse Core Ops, SparseCore 0:
  10.3 51.1 all-gather.1
  256.2 117.8 all-reduce.2
where the time goes:
time: 508 us; the launch traced here: 507 us
  waiting for transfers between devices  280 us (55%)
  blocking collectives  67.9 us (13%)
  local copies, waits for them, and re-layouts  59.1 us (12%)
  matrix products  45.3 us (9%)
  other arithmetic  22.2 us (4%)
  starting transfers between devices  17.4 us (3%)
  between operations  15.1 us (3%)
    unnamed x3, waiting for transfers between devices  117 us
    all_to_all x1, waiting for transfers between devices, local(): lax.all_to_all(block_result.reshape(grouped_rows, current_width, LATENT_W...  105 us
    all_gather x1, waiting for transfers between devices, local(): all_heads = lax.all_gather(query, 'ctx', axis=1, tiled=True)  51.8 us
    unnamed x29, local copies, waits for them, and re-layouts  37.8 us
    all_to_all x1, blocking collectives, local(): lax.all_to_all(outgoing, ('group', 'ctx'), split_axis=0, concat_axis=0, t...  35.5 us
    all_to_all x1, blocking collectives, local(): lax.all_to_all(partial_out.reshape(device_count, slot_span, model_width)....  32.3 us
    dot_general x1, matrix products, local(): jnp.einsum('rqht,rtk->rqhk', probability.astype(jnp.bfloat16), compressed...  13 us
    another operation x1, local copies, waits for them, and re-layouts, local(): block_result.reshape(grouped_rows, current_width, LATENT_WIDTH)[None]  11.5 us
  transfers between devices with their start and end apart: 5, of which 4 were waited for; matrix products, arithmetic and copies ran while one was open for 6% of the time, Pallas kernels for 0%

commit v1 on v0

--- a/solution.py
+++ b/solution.py
@@ -46,7 +46,9 @@
     positions = ctx_index * block_len + jnp.arange(block_len, dtype=jnp.int32)
     live_mask = (positions[None, :] < lengths[:, None])[:, None, None, :]
     compressed_keys = cache[:, :, :LATENT_WIDTH]
-    all_heads = lax.all_gather(query, "ctx", axis=1, tiled=True)
+    all_heads = jnp.concatenate(
+        lax.all_to_all(jnp.stack([query] * lax.axis_size("ctx")), "ctx", 0, 0), axis=1
+    )
     current_width = all_heads.shape[1]
     shaped = all_heads.reshape(request_batch, draft_tokens, current_width, features)
     scores = score_scale * jnp.einsum(

time: 508 us -> 546 us (1.075)
  starting transfers between devices: 17.4 us -> 31.5 us
  waiting for transfers between devices: 280 us -> 292 us
  local copies, waits for them, and re-layouts: 59.1 us -> 71.1 us
    all_to_all x0 -> x1, waiting for transfers between devices: none -> 64.5 us  [local(): lax.all_to_all(jnp.stack([query] * lax.axis_size('ctx')), 'ctx', 0, 0)]
    all_gather x1 -> x0, waiting for transfers between devices: 51.8 us -> none  [local(): all_heads = lax.all_gather(query, 'ctx', axis=1, tiled=True)]
    another operation x0 -> x2, local copies, waits for them, and re-layouts: none -> 14.8 us  [the longest x1 9.11 us: local(): all_heads.reshape(request_batch, draft_tokens, current_width, features)]
    all_to_all x0 -> x1, starting transfers between devices: none -> 9.61 us  [local(): lax.all_to_all(jnp.stack([query] * lax.axis_size('ctx')), 'ctx', 0, 0)]
    all_gather x1 -> x0, local copies, waits for them, and re-layouts: 8.67 us -> none  [local(): all_heads = lax.all_gather(query, 'ctx', axis=1, tiled=True)]
    reshape x0 -> x1, local copies, waits for them, and re-layouts: none -> 7.56 us  [local(): jnp.concatenate(lax.all_to_all(jnp.stack([query] * lax.axis_size('ctx')),...]
    unnamed x29 -> x30, local copies, waits for them, and re-layouts: 37.8 us -> 36.2 us
    unnamed x3 -> x2, waiting for transfers between devices: 117 us -> 118 us
  transfers between devices with their start and end apart: 5 -> 5, of which waited for: 4 -> 4; matrix products, arithmetic and copies ran while one was open for 6% -> 5% of each run, Pallas kernels for 0% -> 0%
where the time goes in v1:
time: 546 us; the launch traced here: 545 us
  waiting for transfers between devices  292 us (53%)
  local copies, waits for them, and re-layouts  71.1 us (13%)
  blocking collectives  67.9 us (12%)
  matrix products  45 us (8%)
  starting transfers between devices  31.5 us (6%)
  other arithmetic  21.6 us (4%)
  between operations  15.1 us (3%)
    unnamed x2, waiting for transfers between devices  118 us
    all_to_all x1, waiting for transfers between devices, local(): lax.all_to_all(block_result.reshape(grouped_rows, current_width, LATENT_W...  105 us
    all_to_all x1, waiting for transfers between devices, local(): lax.all_to_all(jnp.stack([query] * lax.axis_size('ctx')), 'ctx', 0, 0)  64.5 us
    unnamed x30, local copies, waits for them, and re-layouts  36.2 us
    all_to_all x1, blocking collectives, local(): lax.all_to_all(outgoing, ('group', 'ctx'), split_axis=0, concat_axis=0, t...  35.5 us
    all_to_all x1, blocking collectives, local(): lax.all_to_all(partial_out.reshape(device_count, slot_span, model_width)....  32.3 us
    dot_general x1, matrix products, local(): jnp.einsum('rqht,rtk->rqhk', probability.astype(jnp.bfloat16), compressed...  13 us
    another operation x1, local copies, waits for them, and re-layouts, local(): block_result.reshape(grouped_rows, current_width, LATENT_WIDTH)[None]  11.5 us
  transfers between devices with their start and end apart: 5, of which 4 were waited for; matrix products, arithmetic and copies ran while one was open for 5% of the time, Pallas kernels for 0%

profile of v1, /device:TPU:1, one launch (start us, length us, event | category | flops | bytes accessed | tf_op | source)
XLA Modules:
  0.0 544.6 jit_solution(7461399432018236211)
XLA Ops:
  7.2 5.7 %stack.2 = bf16[32,32,4,576]{3,2,1,0:T(4,128)(2,1)} broadcast(bf16[32,4,576]{2,1,0:T(4,128)(2,1)} %param.13), dimensions={1,2,3} | broadcast | bytes 4866048 | tf_op jit(solution)/shard_map/stack | solution.py:50
  12.9 9.6 %all-to-all-start = ((bf16[32,32,4,576]{3,2,1,0:T(4,128)(2,1)}), bf16[32,32,4,576]{3,2,1,0:T(4,128)(2,1)}, u32[]{:S(2)}, u32[]{:S(2)}) async-start(bf16[32,32,4,576]{3,2,1,0:T(4,128)(2,1)} %stack.2), calls=%async_computation | async-start | bytes 10485760 | tf_op jit(solution)/shard_map/all_to_all | solution.py:50
  22.6 64.5 %all-to-all-done = bf16[32,32,4,576]{3,2,1,0:T(4,128)(2,1)} async-done(((bf16[32,32,4,576]{3,2,1,0:T(4,128)(2,1)}), bf16[32,32,4,576]{3,2,1,0:T(4,128)(2,1)}, u32[]{:S(2)}, u32[]{:S(2)}) %all-to-all-start) | async-done | bytes 4718624 | tf_op jit(solution)/shard_map/all_to_all | solution.py:50
  87.1 7.6 %copy.86 = bf16[32,32,4,576]{3,2,1,0:T(4,128)(2,1)} copy(bf16[32,32,4,576]{3,2,0,1:T(4,128)(2,1)} %bitcast) | data formatting | bytes 9437184 | tf_op jit(solution)/shard_map/reshape | solution.py:49
  94.6 9.1 %reshape_reshape.3 = bf16[8,4,128,576]{3,2,1,0:T(8,128)(2,1)} reshape(bf16[32,32,4,576]{3,2,1,0:T(4,128)(2,1)} %copy.86) | data formatting | bytes 9437184 | tf_op jit(solution)/shard_map/reshape;reshape | solution.py:53
  103.7 10.7 %select_reduce_fusion = (f32[8,4,128]{2,1,0:T(4,128)S(1)}, f32[8,4,128,1024]{3,2,1,0:T(8,128)S(1)}) fusion(pred[8,1024]{1,0:T(8,128)(4,1)S(1)} %broadcast_compare_fusion, bf16[8,4,128,576]{3,2,1,0:T(8,128)(2,1)} %reshape_reshape.3, bf16[8,1024,576]{1,2,0:T(8,128)(2,1)} %param.14), kind=kOutput, calls=%fused_computation.1 | convolution fusion | flops 4844417024 | bytes 30957568 | tf_op jit(solution)/shard_map/rqhd,rtd->rqht/dot_general | solution.py:54
  114.4 4.4 fusion
  118.9 1.3 copy-done.1
  120.2 0.5 broadcast.320
  120.8 0.8 reduce.9
  121.6 0.7 reshape.423
  122.3 9.8 %all-to-all-start.3 = ((f32[32,1,128]{2,1,0:T(1,128)}), f32[32,1,128]{2,1,0:T(1,128)S(1)}, u32[]{:S(2)}, u32[]{:S(2)}) async-start(f32[32,1,128]{2,1,0:T(1,128)} %reshape.423), calls=%async_computation.3 | async-start | bytes 32768 | tf_op jit(solution)/shard_map/all_to_all | solution.py:74
  132.1 0.8 reduce.11
  132.9 0.7 reshape.421
  133.6 5.3 all-to-all-done.3
  138.9 4.1 all-to-all-start.1
  143.1 13.0 %fusion.4 = f32[8,4,128,512]{3,2,1,0:T(8,128)} fusion(f32[8,4,128,1024]{3,2,1,0:T(8,128)} %copy-done.1, bf16[8,1024,576]{1,2,0:T(8,128)(2,1)} %param.14, f32[8,4,128]{2,1,0:T(4,128)S(1)} %get-tuple-element.13, pred[8,1024]{1,0:T(8,128)(4,1)S(1)} %broadcast_compare_fusion), kind=kOutput, calls=%fused_computation.7 | convolution fusion | flops 4311744512 | bytes 33579008 | tf_op jit(solution)/shard_map/rqht,rtk->rqhk/dot_general | solution.py:60
  156.0 11.5 %copy.90 = f32[1,32,128,512]{3,1,0,2:T(8,128)} copy(f32[1,32,128,512]{3,2,1,0:T(8,128)} %bitcast.109) | data formatting | bytes 16777216 | tf_op jit(solution)/shard_map/broadcast_in_dim;reshape | solution.py:82
  167.5 7.7 %all-to-all-start.2 = ((f32[1,32,128,512]{3,1,0,2:T(8,128)}), f32[1,32,128,512]{3,1,0,2:T(8,128)}, u32[]{:S(2)}, u32[]{:S(2)}) async-start(f32[1,32,128,512]{3,1,0,2:T(8,128)} %copy.90), calls=%async_computation.2 | async-start | bytes 16777216 | tf_op jit(solution)/shard_map/all_to_all | solution.py:81
  175.2 0.3 all-reduce.3.cloned.1.call-start
  175.5 1.0 select_reduce_fusion.1
  176.5 0.7 reduce.10
  177.4 0.7 reduce.12
  178.6 105.1 %all-to-all-done.2 = f32[1,32,128,512]{3,1,0,2:T(8,128)} async-done(((f32[1,32,128,512]{3,1,0,2:T(8,128)}), f32[1,32,128,512]{3,1,0,2:T(8,128)}, u32[]{:S(2)}, u32[]{:S(2)}) %all-to-all-start.2) | async-done | bytes 8388640 | tf_op jit(solution)/shard_map/all_to_all | solution.py:81
  283.7 3.8 multiply_reduce_fusion
  287.6 0.2 copy.91
  287.8 0.5 fusion.22
  288.3 0.2 fusion.29
  288.6 5.3 convolution_convert_fusion.1
  293.9 0.6 dynamic-slice
  294.5 117.6 %all-reduce.3.cloned.1.call-done = bf16[32,7168]{1,0:T(8,128)(2,1)} async-done(((bf16[32,7168]{1,0:T(8,128)(2,1)}), bf16[32,7168]{1,0:T(8,128)(2,1)}) %all-reduce.3.cloned.1.call-update) | async-done | bytes 458768
  412.1 2.8 multiply_reduce_fusion.2
  415.7 0.2 fusion.33
  415.9 0.7 select_reduce_fusion.2
  416.6 0.6 multiply_divide_fusion
  417.4 0.3 fusion.14
  417.7 0.5 broadcast.324
  418.2 2.7 reduce.13
  420.9 4.6 reshape.425
  425.5 35.5 %all_to_all.69 = bf16[128,2,3584]{2,1,0:T(2,128)(2,1)} all-to-all(bf16[128,2,3584]{2,1,0:T(2,128)(2,1)S(1)} %reshape.425), channel_id=1, replica_groups=mesh['group'=4,'ctx'=32] {'group','ctx'}, dimensions={0} | all-to-all | bytes 3670016 | tf_op jit(solution)/shard_map/all_to_all | solution.py:163
  461.0 11.5 %reshape.426 = bf16[128,1,7168]{2,1,0:T(2,128)(2,1)} reshape(bf16[128,2,3584]{2,1,0:T(2,128)(2,1)} %all_to_all.69) | data formatting | bytes 3670016
  472.5 3.9 fusion.19
  476.5 6.3 %fusion.12 = bf16[128,1,7168]{2,0,1:T(8,128)(2,1)S(1)} fusion(bf16[256,7168]{1,0:T(8,128)(2,1)} %param.25, bf16[7168,256]{1,0:T(8,128)(2,1)} %param.24, bf16[128,1,7168]{2,1,0:T(2,128)(2,1)} %reshape.426, f32[128,256]{1,0:T(8,128)S(1)} %fusion.19), kind=kOutput, calls=%fused_computation.15 | convolution fusion | flops 940638208 | bytes 11141120 | tf_op jit(solution)/shard_map/dot_general | solution.py:20
  482.8 2.7 reduce.14
  485.5 4.6 reshape.427
  490.1 32.3 %all_to_all.70 = bf16[128,2,3584]{2,1,0:T(2,128)(2,1)} all-to-all(bf16[128,2,3584]{2,1,0:T(2,128)(2,1)S(1)} %reshape.427), channel_id=1, replica_groups=mesh['group'=4,'ctx'=32] {'group','ctx'}, dimensions={0} | all-to-all | bytes 3670016 | tf_op jit(solution)/shard_map/all_to_all | solution.py:168
  522.4 11.5 %reshape.428 = bf16[128,1,7168]{2,1,0:T(2,128)(2,1)} reshape(bf16[128,2,3584]{2,1,0:T(2,128)(2,1)} %all_to_all.70) | data formatting | bytes 3670016
  533.9 3.8 fusion.13
  (42 shorter events, 1.3 us)
Async XLA Ops:
  7.2 281.1 %copy-start = (bf16[4,512,128]{2,1,0:T(8,128)(2,1)S(1)}, bf16[4,512,128]{2,1,0:T(8,128)(2,1)}, u32[]{:S(2)}) copy-start(bf16[4,512,128]{2,1,0:T(8,128)(2,1)} %param.17) | copy-start | bytes 1572868
  12.9 9.6 %copy-start.7 = (s32[8]{0:T(128)S(1)}, s32[8]{0:T(128)}, u32[]{:S(2)}) copy-start(s32[8]{0:T(128)} %param.16) | copy-start | bytes 100
  12.9 74.2 %all-to-all-start = ((bf16[32,32,4,576]{3,2,1,0:T(4,128)(2,1)}), bf16[32,32,4,576]{3,2,1,0:T(4,128)(2,1)}, u32[]{:S(2)}, u32[]{:S(2)}) async-start(bf16[32,32,4,576]{3,2,1,0:T(4,128)(2,1)} %stack.2), calls=%async_computation | async-start | bytes 10485760 | tf_op jit(solution)/shard_map/all_to_all | solution.py:50
  114.4 5.7 %copy-start.1 = (f32[8,4,128,1024]{3,2,1,0:T(8,128)}, f32[8,4,128,1024]{3,2,1,0:T(8,128)S(1)}, u32[]{:S(2)}) copy-start(f32[8,4,128,1024]{3,2,1,0:T(8,128)S(1)} %get-tuple-element.14) | copy-start | bytes 50331652
  122.3 16.7 %all-to-all-start.3 = ((f32[32,1,128]{2,1,0:T(1,128)}), f32[32,1,128]{2,1,0:T(1,128)S(1)}, u32[]{:S(2)}, u32[]{:S(2)}) async-start(f32[32,1,128]{2,1,0:T(1,128)} %reshape.423), calls=%async_computation.3 | async-start | bytes 32768 | tf_op jit(solution)/shard_map/all_to_all | solution.py:74
  138.9 28.6 %all-to-all-start.1 = ((f32[32,1,128]{2,1,0:T(1,128)}), f32[32,1,128]{2,1,0:T(1,128)S(1)}, u32[]{:S(2)}, u32[]{:S(2)}) async-start(f32[32,1,128]{2,1,0:T(1,128)} %reshape.421), calls=%async_computation.1 | async-start | bytes 32768 | tf_op jit(solution)/shard_map/all_to_all | solution.py:67
  167.5 8.0 %copy-start.2 = (bf16[32,576]{1,0:T(8,128)(2,1)S(1)}, bf16[32,576]{1,0:T(8,128)(2,1)}, u32[]{:S(2)}) copy-start(bf16[32,576]{1,0:T(8,128)(2,1)} %param.15) | copy-start | bytes 110596
  167.5 8.1 %copy-start.3 = (bf16[32,4,576]{2,1,0:T(4,128)(2,1)S(1)}, bf16[32,4,576]{2,1,0:T(4,128)(2,1)}, u32[]{:S(2)}) copy-start(bf16[32,4,576]{2,1,0:T(4,128)(2,1)} %param.13) | copy-start | bytes 442372
  167.5 116.2 %all-to-all-start.2 = ((f32[1,32,128,512]{3,1,0,2:T(8,128)}), f32[1,32,128,512]{3,1,0,2:T(8,128)}, u32[]{:S(2)}, u32[]{:S(2)}) async-start(f32[1,32,128,512]{3,1,0,2:T(8,128)} %copy.90), calls=%async_computation.2 | async-start | bytes 16777216 | tf_op jit(solution)/shard_map/all_to_all | solution.py:81
  175.2 236.9 %all-reduce.3.cloned.1.call-start = ((), (), s32[]{:S(2)}) async-start(), calls=%async_computation.6 | async-start | bytes 917504
  288.5 5.4 copy-start.9
  288.5 123.6 %copy-start.4 = (bf16[1,7168]{1,0:T(2,128)(2,1)S(1)}, bf16[1,7168]{1,0:T(2,128)(2,1)}, u32[]{:S(2)}) copy-start(bf16[1,7168]{1,0:T(2,128)(2,1)} %param.19) | copy-start | bytes 43012
  288.5 127.1 %copy-start.5 = (f32[7168]{0:T(1024)S(1)}, f32[7168]{0:T(1024)}, u32[]{:S(2)}) copy-start(f32[7168]{0:T(1024)} %param.20) | copy-start | bytes 86020
  288.5 127.2 %copy-start.8 = (bf16[7168,16]{0,1:T(8,128)(2,1)S(1)}, bf16[7168,16]{0,1:T(8,128)(2,1)}, u32[]{:S(2)}) copy-start(bf16[7168,16]{0,1:T(8,128)(2,1)} %param.21) | copy-start | bytes 688132
  288.6 127.4 %copy-start.6 = (s32[1,8]{1,0:T(1,128)S(1)}, s32[1,8]{1,0:T(1,128)}, u32[]{:S(2)}) copy-start(s32[1,8]{1,0:T(1,128)} %param.22) | copy-start | bytes 100
Sparse Core Ops, SparseCore 0:
  294.0 118.0 all-reduce.2
